TPU v7x, 32 devices: a whole 2x2x4 slice. The times are simulated.
32 devices in a mesh: row: 4 (over y, core), col: 8 (over z, x).
Axes of the slice: x: 2, y: 2, z: 4, core: 2. Of those that a mesh axis runs over, the one named last changes fastest.
Arguments:
- factor: float32 [6, 2048, 6, 2048], P(None, 'row', None, 'col'), may hold values from -0.0625 to 0.0625
- diag_inv: float32 [6, 2048, 2048], P(None, None, 'row'), may hold values from -2 to 2, as said below
- structure: int32 [6, 6, 16], P(None, None, 'row'), may hold values 0 or 1
- parent: int32 [6], replicated, may hold values from 1 to 6, as said below
- post: float32 [6, 2048, 64], P(None, 'row', 'col'), may hold values from -6 to 6
Outputs:
- mean_x: float32 [6, 2048, 64], P(None, 'row', 'col')
- variance: float32 [6, 2048], P(None, 'row')
Inputs may be any that keep to these rules, and one draw needn't show every extreme that they name: parent[s] > s for s < 5, and parent[5] = 6; every supernode has at most 2 ancestors, and some supernode has exactly that many. The diagonal of each diag_inv[s] lies in 0.5 to 2.
All inputs are finite; a program needn't handle non-finite values. No bound on the sum of `structure` on one device may be relied on, other than what follows from the above.
Results may differ from a plain program's by a relative error of at most 0.00014.
Values sent between devices are 32-bit elements; how exact they have to be, the bound alone decides.
A program may use at most 192 MiB of HBM per device.

v0:
```python
import jax
import jax.numpy as jnp
from jax import lax
from jax.sharding import PartitionSpec as P

HIGH = lax.Precision.HIGH


def product(left, right):
    return jnp.dot(left, right, precision=HIGH, preferred_element_type=jnp.float32)


def body(factor, diag_inv, structure, parent, post):
    super_count = factor.shape[0]
    row_width = factor.shape[1]
    col_width = factor.shape[3]
    full_width = diag_inv.shape[1]
    row_at = lax.axis_index("row")
    col_at = lax.axis_index("col")
    last = super_count - 1
    block_rows = row_width // structure.shape[2]
    extended = jnp.concatenate([parent, jnp.full((1,), super_count, jnp.int32)])
    first_at = parent
    second_at = extended[parent]

    def pick(current_sup, target):
        clamped = jnp.minimum(target, last)
        block = lax.dynamic_index_in_dim(factor[:, :, current_sup, :], clamped, 0, keepdims=False)
        flags = lax.dynamic_index_in_dim(structure[current_sup], clamped, 0, keepdims=False)
        flags = jnp.where(target < super_count, flags.astype(jnp.float32), 0.0)
        return block * jnp.repeat(flags, block_rows)[:, None]

    blocks = [None] * super_count
    for current_sup in range(last - 1, -1, -1):
        mine = jnp.concatenate(
            [pick(current_sup, first_at[current_sup]), pick(current_sup, second_at[current_sup])],
            axis=0,
        )
        blocks[current_sup] = lax.all_gather(mine, "col", axis=1, tiled=True)
    own_cols = row_at * row_width + jnp.arange(row_width, dtype=jnp.int32)
    rows_full = jnp.arange(full_width, dtype=jnp.int32)
    keep = rows_full[:, None] >= own_cols[None, :]
    lower = [jnp.where(keep, diag_inv[s], 0.0) for s in range(super_count)]
    unit_rows = col_at * col_width + jnp.arange(col_width, dtype=jnp.int32)
    own = lax.dynamic_slice_in_dim(diag_inv, col_at * col_width, col_width, axis=1)
    own = jnp.where((unit_rows[:, None] >= own_cols[None, :])[None], own, 0.0)
    gathered = jnp.swapaxes(lax.all_gather(post, "row", axis=1, tiled=True), 1, 2)

    def take(stacked, target):
        return lax.dynamic_index_in_dim(stacked, jnp.minimum(target, last), 0, keepdims=False)

    rhs = jnp.stack([product(gathered[s], lower[s]) for s in range(super_count)])

    def solve(current_sup, unit_part, rhs_part):
        summed = lax.psum(jnp.concatenate([unit_part, rhs_part], axis=0), "row")
        right = jnp.concatenate(
            [-summed[:col_width], gathered[current_sup] - summed[col_width:]], axis=0
        )
        fresh = product(right, lower[current_sup])
        return (fresh[:col_width], fresh[col_width:])

    near = [jnp.zeros((col_width, row_width), jnp.float32)] * super_count
    means = [rhs[s] for s in range(super_count)]
    for s in range(last - 1, -1, -1):
        one, two = (first_at[s], second_at[s])
        unit_part = product(take(own, one), blocks[s][:row_width])
        rhs_part = product(jnp.concatenate([take(rhs, one), take(rhs, two)], axis=1), blocks[s])
        near[s], means[s] = solve(s, unit_part, rhs_part)
    near_all = jnp.stack(near)
    rhs = jnp.stack(means)
    far = [None] * super_count
    for s in range(last - 1, -1, -1):
        one, two = (first_at[s], second_at[s])
        selected = jnp.concatenate(
            [
                jnp.concatenate([take(near_all, one), take(own, two)], axis=1),
                jnp.concatenate([take(rhs, one), take(rhs, two)], axis=1),
            ],
            axis=0,
        )
        both = product(selected, blocks[s])
        far[s], means[s] = solve(s, both[:col_width], both[col_width:])
    squares = []
    for s in range(super_count):
        total = jnp.sum(own[s] * own[s], axis=0)
        if s < last:
            total = total + jnp.sum(near[s] * near[s], axis=0) + jnp.sum(far[s] * far[s], axis=0)
        squares.append(total)
    variance = lax.psum(jnp.stack(squares), "col")
    mean_x = jnp.swapaxes(jnp.stack(means), 1, 2)
    return (mean_x, variance)


def solution(mesh):
    return jax.shard_map(
        body,
        mesh=mesh,
        in_specs=(
            P(None, "row", None, "col"),
            P(None, None, "row"),
            P(None, None, "row"),
            P(),
            P(None, "row", "col"),
        ),
        out_specs=(P(None, "row", "col"), P(None, "row")),
        check_vma=False,
    )
```

profile of v0, /device:TPU:0, one launch (start us, length us, event | category | flops | bytes accessed | tf_op | source)
XLA Modules:
  0.0 1189.7 jit_solution(15968273963925713293)
XLA Ops:
  17.9 11.0 fusion.291
  51.5 8.9 all_gather.19
  84.9 75.8 %all-gather.8.cloned.1.call-done = f32[1024,2048]{1,0:T(8,128)} async-done(((f32[1024,256]{1,0:T(8,128)}), f32[1024,2048]{1,0:T(8,128)}) %all-gather.8.cloned.1.call-update) | async-done | bytes 8388624 | tf_op jit(solution)/shard_map/all_gather | solution.py:39
  165.0 5.9 fusion.204
  172.4 113.5 %all-gather.10.cloned.1.call-done = f32[1024,2048]{1,0:T(8,128)} async-done(((f32[1024,256]{1,0:T(8,128)}), f32[1024,2048]{1,0:T(8,128)}) %all-gather.10.cloned.1.call-update) | async-done | bytes 8388624 | tf_op jit(solution)/shard_map/all_gather | solution.py:39
  290.2 5.7 fusion.208
  297.4 113.8 %all-gather.12.cloned.1.call-done = f32[1024,2048]{1,0:T(8,128)} async-done(((f32[1024,256]{1,0:T(8,128)}), f32[1024,2048]{1,0:T(8,128)}) %all-gather.12.cloned.1.call-update) | async-done | bytes 8388624 | tf_op jit(solution)/shard_map/all_gather | solution.py:39
  415.4 5.7 fusion.212
  422.6 113.6 %all-gather.14.cloned.1.call-done = f32[1024,2048]{1,0:T(8,128)} async-done(((f32[1024,256]{1,0:T(8,128)}), f32[1024,2048]{1,0:T(8,128)}) %all-gather.14.cloned.1.call-update) | async-done | bytes 8388624 | tf_op jit(solution)/shard_map/all_gather | solution.py:39
  540.4 6.1 fusion.216
  548.1 113.2 %all-gather.6.cloned.1.call-done = f32[1024,2048]{1,0:T(8,128)} async-done(((f32[1024,256]{1,0:T(8,128)}), f32[1024,2048]{1,0:T(8,128)}) %all-gather.6.cloned.1.call-update) | async-done | bytes 8388624 | tf_op jit(solution)/shard_map/all_gather | solution.py:39
  665.5 5.5 fusion.200
  675.0 188.1 %all-reduce.7.cloned.1.call-done = (f32[264,2048]{1,0:T(8,128)}, f32[264,2048]{1,0:T(8,128)}, f32[264,2048]{1,0:T(8,128)}, f32[264,2048]{1,0:T(8,128)}, f32[264,2048]{1,0:T(8,128)}) async-done(((f32[264,2048]{1,0:T(8,128)}, f32[264,2048]{1,0:T(8,128)}, f32[264,2048]{1,0:T(8,128)}, f32[264,2048]{1,0:T(8,128)}, f32[264,2048]{1,0:T(8,128)}), (f32[264,2048]{1,0:T(8,128)}, f32[264,2048]{1,0:T(8,128)}, ...) | async-done | bytes 10813456 | tf_op jit(solution)/shard_map/psum | solution.py:55
  887.0 4.4 fusion.43
  893.8 6.0 fusion.139
  899.9 5.8 fusion.147
  905.8 5.8 fusion.155
  911.6 6.1 fusion.163
  917.7 5.8 fusion.171
  923.9 192.1 %all-reduce.5.cloned.1.call-done = (f32[264,2048]{1,0:T(8,128)}, f32[264,2048]{1,0:T(8,128)}, f32[264,2048]{1,0:T(8,128)}, f32[264,2048]{1,0:T(8,128)}, f32[264,2048]{1,0:T(8,128)}) async-done(((f32[264,2048]{1,0:T(8,128)}, f32[264,2048]{1,0:T(8,128)}, f32[264,2048]{1,0:T(8,128)}, f32[264,2048]{1,0:T(8,128)}, f32[264,2048]{1,0:T(8,128)}), (f32[264,2048]{1,0:T(8,128)}, f32[264,2048]{1,0:T(8,128)}, ...) | async-done | bytes 10813456 | tf_op jit(solution)/shard_map/psum | solution.py:55
  1127.0 4.5 fusion.42
  1135.9 4.3 fusion.38
  1140.3 4.3 fusion.36
  1144.9 37.7 %psum.87 = f32[6,512]{1,0:T(8,128)} all-reduce(f32[6,512]{1,0:T(8,128)S(1)} %stack.112), channel_id=1, replica_groups=mesh['row'=4,'col'=8] {'col'}, use_global_device_ids=true, to_apply=%region_26.27 | all-reduce | flops 3072 | bytes 24576 | tf_op jit(solution)/shard_map/psum | solution.py:89
  (208 shorter events, 118.2 us)
Async XLA Ops:
  7.2 153.6 %all-gather.8.cloned.1.call-start = ((), (), s32[]{:S(2)}) async-start(), calls=%async_computation.1 | async-start | bytes 9437184 | tf_op jit(solution)/shard_map/all_gather | solution.py:39
  32.8 253.2 %all-gather.10.cloned.1.call-start = ((), (), s32[]{:S(2)}) async-start(), calls=%async_computation.2 | async-start | bytes 9437184 | tf_op jit(solution)/shard_map/all_gather | solution.py:39
  35.1 376.1 %all-gather.12.cloned.1.call-start = ((), (), s32[]{:S(2)}) async-start(), calls=%async_computation.3 | async-start | bytes 9437184 | tf_op jit(solution)/shard_map/all_gather | solution.py:39
  45.1 491.1 %all-gather.14.cloned.1.call-start = ((), (), s32[]{:S(2)}) async-start(), calls=%async_computation.4 | async-start | bytes 9437184 | tf_op jit(solution)/shard_map/all_gather | solution.py:39
  47.5 613.8 %all-gather.6.cloned.1.call-start = ((), (), s32[]{:S(2)}) async-start(), calls=%async_computation | async-start | bytes 9437184 | tf_op jit(solution)/shard_map/all_gather | solution.py:39
  51.4 811.7 %all-reduce.7.cloned.1.call-start = ((), (), s32[]{:S(2)}) async-start(), calls=%async_computation.6 | async-start | bytes 21626880 | tf_op jit(solution)/shard_map/psum | solution.py:55
  51.5 30.9 %copy-start.13 = (s32[512]{0:T(512)}, s32[512]{0:T(512)S(1)}, u32[]{:S(2)}) copy-start(s32[512]{0:T(512)S(1)} %iota_add_fusion) | copy-start | bytes 6148
  672.6 443.4 %all-reduce.5.cloned.1.call-start = ((), (), s32[]{:S(2)}) async-start(), calls=%async_computation.5 | async-start | bytes 21626880 | tf_op jit(solution)/shard_map/psum | solution.py:55
  887.0 5.0 slice-start.8
  891.7 8.1 slice-start
  893.8 6.0 slice-start.1
  893.8 6.0 copy-start.11
  893.8 11.9 slice-start.2
  899.8 5.9 slice-start.3
  899.9 5.9 copy-start.10
  899.9 11.7 slice-start.4
  905.7 5.9 slice-start.5
  905.7 5.9 copy-start.9
  905.8 11.9 %slice-start.6 = ((s8[8388608]{0:T(1024)(128)(4,1)}), s8[4194304]{0:T(1024)(128)(4,1)S(1)}, s32[]{:S(2)}) async-start(s8[8388608]{0:T(1024)(128)(4,1)} %bitcast.345), calls=%async_computation.13 | async-start | bytes 8388608
  911.6 6.1 slice-start.7
  911.6 6.1 copy-start.8
  1140.3 4.5 copy-start.26
  1140.3 4.5 copy-start.25
  1144.7 37.8 %copy-start.31 = (f32[6,8,512]{2,1,0:T(8,128)}, f32[6,8,512]{2,1,0:T(8,128)S(1)}, u32[]{:S(2)}) copy-start(f32[6,8,512]{2,1,0:T(8,128)S(1)} %constant_dynamic-update-slice_fusion.7) | copy-start | bytes 294916
  (25 other events, 81.6 us)
Sparse Core Ops, SparseCore 0:
  32.9 127.8 all-gather.7
  162.8 123.1 all-gather.9
  288.0 123.1 all-gather.11
  413.1 123.1 all-gather.13
  538.1 123.1 all-gather.5
  672.7 190.3 all-reduce.6
  923.7 192.3 all-reduce.4
where the time goes:
time: 1190 us
  waiting for transfers between devices  910 us (76%)
  matrix products  144 us (12%)
  blocking collectives  46.6 us (4%)
  other arithmetic  36.7 us (3%)
  between operations  27.8 us (2%)
  local copies, waits for them, and re-layouts  24.2 us (2%)
    all_gather x5, waiting for transfers between devices, body(): blocks[current_sup] = lax.all_gather(mine, 'col', axis=1, tiled=True)  530 us
    psum x2, waiting for transfers between devices, solve(): summed = lax.psum(jnp.concatenate([unit_part, rhs_part], axis=0), 'row')  380 us
    dot_general x31, matrix products, product(): jnp.dot(left, right, precision=HIGH, preferred_element_type=jnp.float32)  144 us
    psum x1, blocking collectives, body(): variance = lax.psum(jnp.stack(squares), 'col')  37.7 us
  transfers between devices with their start and end apart: 7, of which 7 were waited for; matrix products, arithmetic and copies ran while one was open for 7% of the time, Pallas kernels for 0%

commit v1 on v0

--- a/solution.py
+++ b/solution.py
@@ -52,7 +52,9 @@
     rhs = jnp.stack([product(gathered[s], lower[s]) for s in range(super_count)])
 
     def solve(current_sup, unit_part, rhs_part):
-        summed = lax.psum(jnp.concatenate([unit_part, rhs_part], axis=0), "row")
+        own_2 = jnp.concatenate([unit_part, rhs_part], axis=0)
+        parts = lax.all_gather(own_2, "row")
+        summed = jnp.sum(parts, axis=0)
         right = jnp.concatenate(
             [-summed[:col_width], gathered[current_sup] - summed[col_width:]], axis=0
         )

time: 1190 us -> 1400 us (1.18)
  waiting for transfers between devices: 910 us -> 1040 us
  other arithmetic: 36.7 us -> 93.1 us
  matrix products: 144 us -> 159 us
    all_gather x0 -> x10, waiting for transfers between devices: none -> 511 us  [solve(): parts = lax.all_gather(own_2, 'row')]
    psum x2 -> x0, waiting for transfers between devices: 380 us -> none  [solve(): summed = lax.psum(jnp.concatenate([unit_part, rhs_part], axis=0), 'row')]
    reduce_sum x0 -> x10, other arithmetic: none -> 56.5 us  [solve(): summed = jnp.sum(parts, axis=0)]
    dot_general x31, matrix products: 144 us -> 159 us  [product(): jnp.dot(left, right, precision=HIGH, preferred_element_type=jnp.float32)]
  transfers between devices with their start and end apart: 7 -> 15, of which waited for: 7 -> 15; matrix products, arithmetic and copies ran while one was open for 7% -> 13% of each run, Pallas kernels for 0% -> 0%
where the time goes in v1:
time: 1400 us; the launch traced here: 1390 us
  waiting for transfers between devices  1040 us (74%)
  matrix products  159 us (11%)
  other arithmetic  93.1 us (7%)
  blocking collectives  46.2 us (3%)
  between operations  27.1 us (2%)
  local copies, waits for them, and re-layouts  24.7 us (2%)
    all_gather x5, waiting for transfers between devices, body(): blocks[current_sup] = lax.all_gather(mine, 'col', axis=1, tiled=True)  530 us
    all_gather x10, waiting for transfers between devices, solve(): parts = lax.all_gather(own_2, 'row')  511 us
    dot_general x31, matrix products, product(): jnp.dot(left, right, precision=HIGH, preferred_element_type=jnp.float32)  159 us
    reduce_sum x10, other arithmetic, solve(): summed = jnp.sum(parts, axis=0)  56.5 us
    psum x1, blocking collectives, body(): variance = lax.psum(jnp.stack(squares), 'col')  37.7 us
  transfers between devices with their start and end apart: 15, of which 15 were waited for; matrix products, arithmetic and copies ran while one was open for 13% of the time, Pallas kernels for 0%

profile of v1, /device:TPU:0, one launch (start us, length us, event | category | flops | bytes accessed | tf_op | source)
XLA Modules:
  0.0 1392.8 jit_solution(14972160799708784)
XLA Ops:
  16.6 10.9 fusion.291
  50.5 8.5 all_gather.79
  83.6 76.4 %all-gather.34.cloned.1.call-done = f32[1024,2048]{1,0:T(8,128)} async-done(((f32[1024,256]{1,0:T(8,128)}), f32[1024,2048]{1,0:T(8,128)}) %all-gather.34.cloned.1.call-update) | async-done | bytes 8388624 | tf_op jit(solution)/shard_map/all_gather | solution.py:39
  171.7 113.5 %all-gather.32.cloned.1.call-done = f32[1024,2048]{1,0:T(8,128)} async-done(((f32[1024,256]{1,0:T(8,128)}), f32[1024,2048]{1,0:T(8,128)}) %all-gather.32.cloned.1.call-update) | async-done | bytes 8388624 | tf_op jit(solution)/shard_map/all_gather | solution.py:39
  296.7 113.7 %all-gather.30.cloned.1.call-done = f32[1024,2048]{1,0:T(8,128)} async-done(((f32[1024,256]{1,0:T(8,128)}), f32[1024,2048]{1,0:T(8,128)}) %all-gather.30.cloned.1.call-update) | async-done | bytes 8388624 | tf_op jit(solution)/shard_map/all_gather | solution.py:39
  422.3 113.1 %all-gather.28.cloned.1.call-done = f32[1024,2048]{1,0:T(8,128)} async-done(((f32[1024,256]{1,0:T(8,128)}), f32[1024,2048]{1,0:T(8,128)}) %all-gather.28.cloned.1.call-update) | async-done | bytes 8388624 | tf_op jit(solution)/shard_map/all_gather | solution.py:39
  547.0 113.5 %all-gather.26.cloned.1.call-done = f32[1024,2048]{1,0:T(8,128)} async-done(((f32[1024,256]{1,0:T(8,128)}), f32[1024,2048]{1,0:T(8,128)}) %all-gather.26.cloned.1.call-update) | async-done | bytes 8388624 | tf_op jit(solution)/shard_map/all_gather | solution.py:39
  664.7 6.5 fusion.200
  675.5 44.4 %all-gather.44.cloned.1.call-done = f32[1056,2048]{1,0:T(8,128)} async-done(((f32[264,2048]{1,0:T(8,128)}), f32[1056,2048]{1,0:T(8,128)}) %all-gather.44.cloned.1.call-update) | async-done | bytes 8650768 | tf_op jit(solution)/shard_map/all_gather | solution.py:56
  724.4 56.8 %all-gather.42.cloned.1.call-done = f32[1056,2048]{1,0:T(8,128)} async-done(((f32[264,2048]{1,0:T(8,128)}), f32[1056,2048]{1,0:T(8,128)}) %all-gather.42.cloned.1.call-update) | async-done | bytes 8650768 | tf_op jit(solution)/shard_map/all_gather | solution.py:56
  787.2 55.4 %all-gather.40.cloned.1.call-done = f32[1056,2048]{1,0:T(8,128)} async-done(((f32[264,2048]{1,0:T(8,128)}), f32[1056,2048]{1,0:T(8,128)}) %all-gather.40.cloned.1.call-update) | async-done | bytes 8650768 | tf_op jit(solution)/shard_map/all_gather | solution.py:56
  842.6 6.0 reduce_sum.236
  848.5 55.4 %all-gather.38.cloned.1.call-done = f32[1056,2048]{1,0:T(8,128)} async-done(((f32[264,2048]{1,0:T(8,128)}), f32[1056,2048]{1,0:T(8,128)}) %all-gather.38.cloned.1.call-update) | async-done | bytes 8650768 | tf_op jit(solution)/shard_map/all_gather | solution.py:56
  909.8 55.3 %all-gather.36.cloned.1.call-done = f32[1056,2048]{1,0:T(8,128)} async-done(((f32[264,2048]{1,0:T(8,128)}), f32[1056,2048]{1,0:T(8,128)}) %all-gather.36.cloned.1.call-update) | async-done | bytes 8650768 | tf_op jit(solution)/shard_map/all_gather | solution.py:56
  1009.0 9.0 fusion.163
  1018.1 10.4 fusion.155
  1028.6 9.0 fusion.147
  1037.8 9.2 fusion.139
  1047.3 21.2 %all-gather.54.cloned.1.call-done = f32[1056,2048]{1,0:T(8,128)} async-done(((f32[264,2048]{1,0:T(8,128)}), f32[1056,2048]{1,0:T(8,128)}) %all-gather.54.cloned.1.call-update) | async-done | bytes 8650768 | tf_op jit(solution)/shard_map/all_gather | solution.py:56
  1073.0 56.6 %all-gather.52.cloned.1.call-done = f32[1056,2048]{1,0:T(8,128)} async-done(((f32[264,2048]{1,0:T(8,128)}), f32[1056,2048]{1,0:T(8,128)}) %all-gather.52.cloned.1.call-update) | async-done | bytes 8650768 | tf_op jit(solution)/shard_map/all_gather | solution.py:56
  1135.6 55.4 %all-gather.50.cloned.1.call-done = f32[1056,2048]{1,0:T(8,128)} async-done(((f32[264,2048]{1,0:T(8,128)}), f32[1056,2048]{1,0:T(8,128)}) %all-gather.50.cloned.1.call-update) | async-done | bytes 8650768 | tf_op jit(solution)/shard_map/all_gather | solution.py:56
  1196.9 55.3 %all-gather.48.cloned.1.call-done = f32[1056,2048]{1,0:T(8,128)} async-done(((f32[264,2048]{1,0:T(8,128)}), f32[1056,2048]{1,0:T(8,128)}) %all-gather.48.cloned.1.call-update) | async-done | bytes 8650768 | tf_op jit(solution)/shard_map/all_gather | solution.py:56
  1258.1 55.3 %all-gather.46.cloned.1.call-done = f32[1056,2048]{1,0:T(8,128)} async-done(((f32[264,2048]{1,0:T(8,128)}), f32[1056,2048]{1,0:T(8,128)}) %all-gather.46.cloned.1.call-update) | async-done | bytes 8650768 | tf_op jit(solution)/shard_map/all_gather | solution.py:56
  1348.4 37.7 %psum.7 = f32[6,512]{1,0:T(8,128)} all-reduce(f32[6,512]{1,0:T(8,128)S(1)} %stack.112), channel_id=1, replica_groups=mesh['row'=4,'col'=8] {'col'}, use_global_device_ids=true, to_apply=%region_26.27 | all-reduce | flops 3072 | bytes 24576 | tf_op jit(solution)/shard_map/psum | solution.py:91
  (212 shorter events, 217.3 us)
Async XLA Ops:
  7.2 152.8 %all-gather.34.cloned.1.call-start = ((), (), s32[]{:S(2)}) async-start(), calls=%async_computation.4 | async-start | bytes 9437184 | tf_op jit(solution)/shard_map/all_gather | solution.py:39
  16.6 11.0 copy-start.19
  32.3 252.9 %all-gather.32.cloned.1.call-start = ((), (), s32[]{:S(2)}) async-start(), calls=%async_computation.3 | async-start | bytes 9437184 | tf_op jit(solution)/shard_map/all_gather | solution.py:39
  34.7 375.7 %all-gather.30.cloned.1.call-start = ((), (), s32[]{:S(2)}) async-start(), calls=%async_computation.2 | async-start | bytes 9437184 | tf_op jit(solution)/shard_map/all_gather | solution.py:39
  44.2 491.3 %all-gather.28.cloned.1.call-start = ((), (), s32[]{:S(2)}) async-start(), calls=%async_computation.1 | async-start | bytes 9437184 | tf_op jit(solution)/shard_map/all_gather | solution.py:39
  46.5 614.0 %all-gather.26.cloned.1.call-start = ((), (), s32[]{:S(2)}) async-start(), calls=%async_computation | async-start | bytes 9437184 | tf_op jit(solution)/shard_map/all_gather | solution.py:39
  50.5 669.4 %all-gather.44.cloned.1.call-start = ((), (), s32[]{:S(2)}) async-start(), calls=%async_computation.9 | async-start | bytes 10813440 | tf_op jit(solution)/shard_map/all_gather | solution.py:56
  50.5 30.6 %copy-start.7 = (s32[512]{0:T(512)}, s32[512]{0:T(512)S(1)}, u32[]{:S(2)}) copy-start(s32[512]{0:T(512)S(1)} %iota_add_fusion) | copy-start | bytes 6148
  171.7 609.5 %all-gather.42.cloned.1.call-start = ((), (), s32[]{:S(2)}) async-start(), calls=%async_computation.8 | async-start | bytes 10813440 | tf_op jit(solution)/shard_map/all_gather | solution.py:56
  296.7 545.9 %all-gather.40.cloned.1.call-start = ((), (), s32[]{:S(2)}) async-start(), calls=%async_computation.7 | async-start | bytes 10813440 | tf_op jit(solution)/shard_map/all_gather | solution.py:56
  421.9 482.0 %all-gather.38.cloned.1.call-start = ((), (), s32[]{:S(2)}) async-start(), calls=%async_computation.6 | async-start | bytes 10813440 | tf_op jit(solution)/shard_map/all_gather | solution.py:56
  547.0 418.1 %all-gather.36.cloned.1.call-start = ((), (), s32[]{:S(2)}) async-start(), calls=%async_computation.5 | async-start | bytes 10813440 | tf_op jit(solution)/shard_map/all_gather | solution.py:56
  672.7 395.7 %all-gather.54.cloned.1.call-start = ((), (), s32[]{:S(2)}) async-start(), calls=%async_computation.14 | async-start | bytes 10813440 | tf_op jit(solution)/shard_map/all_gather | solution.py:56
  995.1 6.1 slice-start
  1008.6 121.1 %all-gather.52.cloned.1.call-start = ((), (), s32[]{:S(2)}) async-start(), calls=%async_computation.13 | async-start | bytes 10813440 | tf_op jit(solution)/shard_map/all_gather | solution.py:56
  1018.1 173.0 %all-gather.50.cloned.1.call-start = ((), (), s32[]{:S(2)}) async-start(), calls=%async_computation.12 | async-start | bytes 10813440 | tf_op jit(solution)/shard_map/all_gather | solution.py:56
  1028.5 223.7 %all-gather.48.cloned.1.call-start = ((), (), s32[]{:S(2)}) async-start(), calls=%async_computation.11 | async-start | bytes 10813440 | tf_op jit(solution)/shard_map/all_gather | solution.py:56
  1037.6 275.8 %all-gather.46.cloned.1.call-start = ((), (), s32[]{:S(2)}) async-start(), calls=%async_computation.10 | async-start | bytes 10813440 | tf_op jit(solution)/shard_map/all_gather | solution.py:56
  1343.8 4.4 copy-start.24
  1343.8 4.5 copy-start.23
  1343.8 4.5 copy-start.22
  1343.8 4.5 copy-start.21
  1343.8 4.5 copy-start.20
  1348.2 37.8 %copy-start.26 = (f32[6,8,512]{2,1,0:T(8,128)}, f32[6,8,512]{2,1,0:T(8,128)S(1)}, u32[]{:S(2)}) copy-start(f32[6,8,512]{2,1,0:T(8,128)S(1)} %constant_dynamic-update-slice_fusion.7) | copy-start | bytes 294916
  (20 other events, 64.5 us)
Sparse Core Ops, SparseCore 0:
  32.4 127.5 all-gather.33
  162.0 123.1 all-gather.31
  287.2 123.1 all-gather.29
  412.3 123.1 all-gather.27
  537.3 123.1 all-gather.25
  661.9 57.9 all-gather.43
  721.4 59.7 all-gather.41
  782.8 59.7 all-gather.39
  844.1 59.7 all-gather.37
  905.3 59.7 all-gather.35
  1008.7 59.7 all-gather.53
  1069.9 59.7 all-gather.51
  1131.2 59.7 all-gather.49
  1192.4 59.7 all-gather.47
  1253.6 59.7 all-gather.45
